TPU v7x, 32 devices: a whole 2x2x4 slice. The times are simulated.
32 devices in a mesh: ctx: 8 (over z, core), tp: 4 (over y, x).
Axes of the slice: x: 2, y: 2, z: 4, core: 2. Of those that a mesh axis runs over, the one named last changes fastest.
Arguments:
- hidden_rows: bfloat16 [4096, 8192], P('ctx', 'tp'), may hold values from -6 to 6
- w_value: bfloat16 [8192, 8192], P('ctx', 'tp'), may hold values from -0.0625 to 0.0625
- w_gate: bfloat16 [8192, 8192], P('ctx', 'tp'), may hold values from -0.0625 to 0.0625
- state_proj: bfloat16 [4096, 2, 4, 256], P('ctx'), may hold values from -1.5 to 1.5
- rates: float32 [4096, 128], P('ctx', 'tp'), may hold values from 0 to 4.5, as said below
- read_weights: float32 [6, 4096, 128], P(None, 'ctx', 'tp'), may hold values from 0.25 to 2
- prior_state: float32 [128, 64, 256], P('tp'), may hold values from -24 to 24
- skip_weight: float32 [128], P('tp'), may hold values from 0.5 to 2
- norm_gain: float32 [8192], P('tp'), may hold values from 0.25 to 1.75
Outputs:
- layer_out: bfloat16 [4096, 8192], P('ctx', 'tp')
Inputs may be any that keep to these rules, and one draw needn't show every extreme that they name: Positive rates.
All inputs are finite; a program needn't handle non-finite values.
Results may differ from a plain program's by a relative error of at most 0.0085.
Values may be sent and summed in bfloat16 or wider, within the bound.
A program may use at most 128 MiB of HBM per device.

v0:
```python
import jax
import jax.numpy as jnp
from jax import lax
from jax.sharding import PartitionSpec as P

HEAD_DIM = 64
STATE = 256
HPG = 32
LEVELS = 6


def swapped(value, axis, distance):
    return lax.ppermute(value, axis, [(i, i ^ 1 << distance) for i in range(lax.axis_size(axis))])


def on_device(
    hidden_rows,
    w_value,
    w_gate,
    state_proj,
    rates,
    read_weights,
    prior_state,
    skip_weight,
    norm_gain,
):
    tok_rows = rates.shape[0]
    head_count = rates.shape[1]
    level_total = LEVELS - 2
    ctx_size = lax.axis_size("ctx")
    half = ctx_size // 2
    my_block = lax.axis_index("ctx")
    upper_half = my_block // half
    groups = [list(range(half)), list(range(half, ctx_size))]
    across = [(i, (i + half) % ctx_size) for i in range(ctx_size)]
    w_value_half = lax.all_gather(w_value, "ctx", axis=0, tiled=True, axis_index_groups=groups)
    token_part = lax.all_to_all(hidden_rows, "tp", 0, 1, tiled=True)
    depth = token_part.shape[1] // 2
    kept = lax.dynamic_slice_in_dim(token_part, upper_half * depth, depth, 1)
    given = lax.dynamic_slice_in_dim(token_part, (1 - upper_half) * depth, depth, 1)
    taken = lax.ppermute(given, "ctx", across)
    rows = lax.all_gather(jnp.stack([kept, taken]), "tp", axis=1, tiled=True)
    w_gate_half = lax.all_gather(w_gate, "ctx", axis=0, tiled=True, axis_index_groups=groups)

    def project(weight):
        other = jnp.dot(rows[1], weight, preferred_element_type=jnp.float32).astype(jnp.bfloat16)
        back = lax.ppermute(other, "ctx", across)
        mine = jnp.dot(rows[0], weight, preferred_element_type=jnp.float32)
        return (mine + back.astype(jnp.float32)).astype(jnp.bfloat16)

    values_proj = project(w_value_half)
    gates_proj = project(w_gate_half)
    values3 = values_proj.reshape(tok_rows, head_count, HEAD_DIM)
    group_index = lax.axis_index("tp") * head_count // HPG
    write_vec = lax.dynamic_index_in_dim(state_proj[:, 0], group_index, 1, keepdims=False)
    read_vec = lax.dynamic_index_in_dim(state_proj[:, 1], group_index, 1, keepdims=False)
    cum_rate = jnp.cumsum(rates, axis=0)
    scores = lax.dot_general(
        read_vec, write_vec, (((1,), (1,)), ((), ())), preferred_element_type=jnp.float32
    )
    rate_lag = cum_rate.T[:, :, None] - cum_rate.T[:, None, :]
    causal = (jnp.arange(tok_rows)[:, None] >= jnp.arange(tok_rows)[None, :])[None]
    mixing = (
        jnp.where(causal, jnp.exp(-jnp.where(causal, rate_lag, 0.0)), 0.0) * scores[None]
    ).astype(jnp.bfloat16)
    local_out = jnp.einsum("hts,shp->thp", mixing, values3, preferred_element_type=jnp.float32)
    span_total = cum_rate[-1]
    write_weighted = (
        jnp.exp(-(span_total[None] - cum_rate))[:, :, None]
        * write_vec[:, None, :].astype(jnp.float32)
    ).astype(jnp.bfloat16)
    end_state = jnp.einsum(
        "thn,thp->hpn", write_weighted, values3, preferred_element_type=jnp.float32
    )
    agg_state = end_state
    agg_rate = span_total
    start_rate = jnp.zeros((head_count,), jnp.float32)
    tier_components = []
    bits = ctx_size.bit_length() - 1
    for bit_pos in range(bits):
        is_upper = jnp.right_shift(my_block, bit_pos) % 2 == 1
        if bit_pos < bits - 1:
            other_state, other_rate = swapped(
                (agg_state.astype(jnp.bfloat16), agg_rate), "ctx", bit_pos
            )
        else:
            share = head_count // half
            piece = lax.dynamic_slice_in_dim(
                agg_state.astype(jnp.bfloat16), my_block % half * share, share, 0
            )
            piece, other_rate = swapped((piece, agg_rate), "ctx", bit_pos)
            other_state = lax.all_gather(piece, "ctx", axis=0, tiled=True, axis_index_groups=groups)
        other_state = other_state.astype(jnp.float32)
        tier_components.append(
            jnp.where(is_upper, other_state * jnp.exp(-start_rate)[:, None, None], 0.0).astype(
                jnp.bfloat16
            )
        )
        if bit_pos < bits - 1:
            agg_state = jnp.where(
                is_upper,
                other_state * jnp.exp(-agg_rate)[:, None, None] + agg_state,
                agg_state * jnp.exp(-other_rate)[:, None, None] + other_state,
            )
            agg_rate = agg_rate + other_rate
        start_rate = jnp.where(is_upper, start_rate + other_rate, start_rate)
    level_ids = list(range(1, 1 + len(tier_components))) + [level_total + 1]
    prior_part = (jnp.exp(-start_rate)[:, None, None] * prior_state).astype(jnp.bfloat16)
    carried_out = 0.0
    for level, state in zip(level_ids, tier_components + [prior_part]):
        projected = lax.dot_general(
            read_vec, state, (((1,), (2,)), ((), ())), preferred_element_type=jnp.float32
        )
        carried_out = carried_out + read_weights[level][:, :, None] * projected
    carried_out = carried_out * jnp.exp(-cum_rate)[:, :, None]
    mixed_out = (
        read_weights[0][:, :, None] * local_out
        + carried_out
        + skip_weight[None, :, None] * values3.astype(jnp.float32)
    )
    gates3 = gates_proj.reshape(tok_rows, head_count, HEAD_DIM).astype(jnp.float32)
    filtered_result = mixed_out * jax.nn.silu(gates3)
    inverse = lax.rsqrt(jnp.mean(filtered_result * filtered_result, axis=2, keepdims=True) + 1e-05)
    result = filtered_result * inverse * norm_gain.reshape(head_count, HEAD_DIM)[None]
    return result.reshape(tok_rows, head_count * HEAD_DIM).astype(jnp.bfloat16)


def solution(mesh):
    in_specs = (
        P("ctx", "tp"),
        P("ctx", "tp"),
        P("ctx", "tp"),
        P("ctx", None, None, None),
        P("ctx", "tp"),
        P(None, "ctx", "tp"),
        P("tp", None, None),
        P("tp"),
        P("tp"),
    )
    out_specs = P("ctx", "tp")
    return jax.shard_map(
        on_device, mesh=mesh, in_specs=in_specs, out_specs=out_specs, check_vma=False
    )
```

profile of v0, /device:TPU:9, one launch (start us, length us, event | category | flops | bytes accessed | tf_op | source)
XLA Modules:
  0.0 692.2 jit_solution(7974122275637715766)
XLA Ops:
  6.5 3.7 all-to-all-start
  10.4 24.3 %all-to-all-done = bf16[4,128,2048]{2,1,0:T(8,128)(2,1)S(1)} async-done(((bf16[4,128,2048]{2,1,0:T(8,128)(2,1)}), bf16[4,128,2048]{2,1,0:T(8,128)(2,1)S(1)}, u32[]{:S(2)}, u32[]{:S(2)}) %all-to-all-start) | async-done | bytes 2097184 | tf_op jit(solution)/shard_map/all_to_all | solution.py:37
  34.6 1.3 copy-done.2
  36.0 3.0 copy.35
  39.1 2.4 collective-permute-start
  41.5 45.2 %collective-permute-done = bf16[128,4096]{0,1:T(8,128)(2,1)S(1)} collective-permute-done((bf16[128,4096]{0,1:T(8,128)(2,1)S(1)}, bf16[128,4096]{0,1:T(8,128)(2,1)S(1)}, u32[]{:S(2)}, u32[]{:S(2)}) %collective-permute-start) | collective-permute-done | bytes 1048608 | tf_op jit(solution)/shard_map/ppermute | solution.py:41
  86.8 1.5 pad_maximum_fusion
  89.8 86.4 %all-gather.5.cloned.1.call-done = bf16[2,512,4096]{1,2,0:T(8,128)(2,1)} async-done(((bf16[2,128,4096]{1,2,0:T(8,128)(2,1)}), bf16[2,512,4096]{1,2,0:T(8,128)(2,1)}) %all-gather.5.cloned.1.call-update) | async-done | bytes 8388624 | tf_op jit(solution)/shard_map/all_gather | solution.py:42
  176.2 149.6 %all-gather.7.cloned.1.call-done = bf16[4096,2048]{1,0:T(8,128)(2,1)} async-done(((bf16[1024,2048]{1,0:T(8,128)(2,1)}), bf16[4096,2048]{1,0:T(8,128)(2,1)}) %all-gather.7.cloned.1.call-update) | async-done | bytes 16777232 | tf_op jit(solution)/shard_map/all_gather | solution.py:36
  325.8 14.6 %fusion.12 = bf16[512,2048]{1,0:T(8,128)(2,1)} fusion(bf16[4096,2048]{1,0:T(8,128)(2,1)} %all-gather.7.cloned.1.call-done, bf16[2,512,4096]{1,2,0:T(8,128)(2,1)} %all-gather.5.cloned.1.call-done), kind=kOutput, calls=%fused_computation.24 | convolution fusion | flops 8590983168 | bytes 23068672 | tf_op jit(solution)/shard_map/dot_general | solution.py:46
  340.4 2.3 collective-permute-start.1
  345.0 2.4 fusion.50
  348.1 85.4 %collective-permute-done.1 = bf16[512,2048]{1,0:T(8,128)(2,1)} collective-permute-done((bf16[512,2048]{1,0:T(8,128)(2,1)}, bf16[512,2048]{1,0:T(8,128)(2,1)}, u32[]{:S(2)}, u32[]{:S(2)}) %collective-permute-start.1) | collective-permute-done | bytes 2097184 | tf_op jit(solution)/shard_map/ppermute | solution.py:47
  433.5 15.1 %add_convert_fusion.1 = bf16[512,2048]{1,0:T(8,128)(2,1)} fusion(bf16[512,2048]{1,0:T(8,128)(2,1)} %collective-permute-done.1, bf16[4096,2048]{1,0:T(8,128)(2,1)} %all-gather.7.cloned.1.call-done, bf16[2,512,4096]{1,2,0:T(8,128)(2,1)} %all-gather.5.cloned.1.call-done), kind=kOutput, calls=%fused_computation.16 | convolution fusion | flops 8593080320 | bytes 25165824 | tf_op jit(solution)/shard_map/dot_general | solution.py:48
  448.7 4.0 copy.36
  452.6 5.1 fusion.51
  458.1 62.8 %all-gather.11.cloned.1.call-done = bf16[4096,2048]{1,0:T(8,128)(2,1)} async-done(((bf16[1024,2048]{1,0:T(8,128)(2,1)}), bf16[4096,2048]{1,0:T(8,128)(2,1)}) %all-gather.11.cloned.1.call-update) | async-done | bytes 16777232 | tf_op jit(solution)/shard_map/all_gather | solution.py:43
  520.9 14.6 %fusion.13 = bf16[512,2048]{1,0:T(8,128)(2,1)} fusion(bf16[4096,2048]{1,0:T(8,128)(2,1)} %all-gather.11.cloned.1.call-done, bf16[2,512,4096]{1,2,0:T(8,128)(2,1)} %all-gather.5.cloned.1.call-done), kind=kOutput, calls=%fused_computation.25 | convolution fusion | flops 8590983168 | bytes 23068672 | tf_op jit(solution)/shard_map/dot_general | solution.py:46
  535.4 2.3 collective-permute-start.8
  538.9 2.2 fusion.48
  543.9 1.3 fusion.37
  545.6 61.4 %collective-permute-done.5 = f32[32]{0:T(128)S(1)} collective-permute-done((f32[32]{0:T(128)S(1)}, f32[32]{0:T(128)S(1)}, u32[]{:S(2)}, u32[]{:S(2)}) %collective-permute-start.5) | collective-permute-done | bytes 160 | tf_op jit(solution)/shard_map/ppermute | solution.py:13
  607.7 20.8 %collective-permute-done.7 = f32[32]{0:T(128)S(1)} collective-permute-done((f32[32]{0:T(128)S(1)}, f32[32]{0:T(128)S(1)}, u32[]{:S(2)}, u32[]{:S(2)}) %collective-permute-start.7) | collective-permute-done | bytes 160 | tf_op jit(solution)/shard_map/ppermute | solution.py:13
  629.5 3.0 collective-permute-start.6
  632.5 15.3 %fusion.14 = f32[512,2048]{1,0:T(8,128)} fusion(bf16[512,2048]{1,0:T(8,128)(2,1)} %collective-permute-done.8, bf16[4096,2048]{1,0:T(8,128)(2,1)} %all-gather.11.cloned.1.call-done, bf16[2,512,4096]{1,2,0:T(8,128)(2,1)} %all-gather.5.cloned.1.call-done), kind=kOutput, calls=%fused_computation.26 | convolution fusion | flops 8594128896 | bytes 27262976 | tf_op jit(solution)/shard_map/dot_general | solution.py:48
  647.9 12.0 %fusion = f32[32,64,512]{2,1,0:T(8,128)} fusion(bf16[512,32,64]{0,2,1:T(8,128)(2,1)} %bitcast.101, f32[512,512]{1,0:T(8,128)S(1)} %copy-done.5, f32[32,512]{1,0:T(8,128)S(1)} %copy-done.7, pred[512,512]{1,0:T(8,128)(4,1)} %iota_compare_fusion), kind=kOutput, calls=%fused_computation.2 | convolution fusion | flops 1124073472 | bytes 7667712 | tf_op jit(solution)/shard_map/hts,shp->thp/dot_general | solution.py:66
  659.9 5.5 copy.41
  665.4 2.7 fusion.21
  668.1 2.8 fusion.18
  671.0 2.1 fusion.19
  674.1 8.6 %multiply_reduce_fusion = (f32[512,32]{0,1:T(8,128)S(1)}, f32[512,32,64]{0,2,1:T(8,128)S(1)}) fusion(f32[32]{0:T(128)S(1)} %copy-done.17, f32[512,32]{0,1:T(8,128)S(1)} %get-tuple-element.25, f32[512,32]{0,1:T(8,128)S(1)} %copy-done.11, f32[512,32,64]{0,2,1:T(8,128)S(1)} %fusion.19, f32[512,32]{0,1:T(8,128)S(1)} %copy-done.12, f32[512,32,64]{0,2,1:T(8,128)} %fusion.18, ...), kind=kOutput, calls=%fused_computation.14 | convolution fusion | flops 558874624 | bytes 30081280 | tf_op jit(solution)/shard_map/dot_general | solution.py:111
  683.3 2.4 copy.42
  (79 shorter events, 12.5 us)
Async XLA Ops:
  6.5 336.2 %copy-start = (f32[512,32]{0,1:T(8,128)S(1)}, f32[512,32]{0,1:T(8,128)}, u32[]{:S(2)}) copy-start(f32[512,32]{0,1:T(8,128)} %param.13) | copy-start | bytes 196612
  6.5 28.1 %all-to-all-start = ((bf16[4,128,2048]{2,1,0:T(8,128)(2,1)}), bf16[4,128,2048]{2,1,0:T(8,128)(2,1)S(1)}, u32[]{:S(2)}, u32[]{:S(2)}) async-start(bf16[4,128,2048]{2,1,0:T(8,128)(2,1)} %bitcast.99), calls=%async_computation | async-start | bytes 4194304 | tf_op jit(solution)/shard_map/all_to_all | solution.py:37
  10.3 165.9 %all-gather.5.cloned.1.call-start = ((), (), s32[]{:S(2)}) async-start(), calls=%async_computation.1 | async-start | bytes 10485760 | tf_op jit(solution)/shard_map/all_gather | solution.py:42
  34.6 1.3 copy-start.2
  39.1 47.6 %collective-permute-start = (bf16[128,4096]{0,1:T(8,128)(2,1)S(1)}, bf16[128,4096]{0,1:T(8,128)(2,1)S(1)}, u32[]{:S(2)}, u32[]{:S(2)}) collective-permute-start(bf16[128,4096]{0,1:T(8,128)(2,1)S(1)} %get-tuple-element.16), channel_id=1, source_target_pairs={{0,16},{4,20},{8,24},{12,28},{16,0},{20,4},{24,8},{28,12},{1,17},{... | collective-permute-start | bytes 3145736 | tf_op jit(solution)/shard_map/ppermute | solution.py:41
  88.3 237.6 %all-gather.7.cloned.1.call-start = ((), (), s32[]{:S(2)}) async-start(), calls=%async_computation.2 | async-start | bytes 20971520 | tf_op jit(solution)/shard_map/all_gather | solution.py:36
  89.0 431.8 %all-gather.11.cloned.1.call-start = ((), (), s32[]{:S(2)}) async-start(), calls=%async_computation.4 | async-start | bytes 20971520 | tf_op jit(solution)/shard_map/all_gather | solution.py:43
  89.8 581.2 %all-gather.9.cloned.1.call-start = ((), (), s32[]{:S(2)}) async-start(), calls=%async_computation.3 | async-start | bytes 1310720 | tf_op jit(solution)/shard_map/all_gather | solution.py:92
  340.4 93.1 %collective-permute-start.1 = (bf16[512,2048]{1,0:T(8,128)(2,1)}, bf16[512,2048]{1,0:T(8,128)(2,1)}, u32[]{:S(2)}, u32[]{:S(2)}) collective-permute-start(bf16[512,2048]{1,0:T(8,128)(2,1)} %fusion.12), channel_id=1, source_target_pairs={{0,16},{4,20},{8,24},{12,28},{16,0},{20,4},{24,8},{28,12},{1,17},{... | collective-permute-start | bytes 6291464 | tf_op jit(solution)/shard_map/ppermute | solution.py:47
  457.7 80.7 %copy-start.15 = (f32[2048]{0:T(1024)S(1)}, f32[2048]{0:T(1024)}, u32[]{:S(2)}) copy-start(f32[2048]{0:T(1024)} %param.17) | copy-start | bytes 24580
  457.7 81.2 %collective-permute-start.2 = (bf16[32,64,256]{2,1,0:T(8,128)(2,1)}, bf16[32,64,256]{2,1,0:T(8,128)(2,1)S(1)}, u32[]{:S(2)}, u32[]{:S(2)}) collective-permute-start(bf16[32,64,256]{2,1,0:T(8,128)(2,1)} %get-tuple-element.31), channel_id=1, source_target_pairs={{0,4},{4,0},{8,12},{12,8},{16,20},{20,16},{24,28},{28,24},{1,5},{5... | collective-permute-start | bytes 3145736 | tf_op jit(solution)/shard_map/ppermute | solution.py:13
  535.4 97.1 %collective-permute-start.8 = (bf16[512,2048]{1,0:T(8,128)(2,1)}, bf16[512,2048]{1,0:T(8,128)(2,1)}, u32[]{:S(2)}, u32[]{:S(2)}) collective-permute-start(bf16[512,2048]{1,0:T(8,128)(2,1)} %fusion.13), channel_id=1, source_target_pairs={{0,16},{4,20},{8,24},{12,28},{16,0},{20,4},{24,8},{28,12},{1,17},{... | collective-permute-start | bytes 6291464 | tf_op jit(solution)/shard_map/ppermute | solution.py:47
  537.8 1.2 collective-permute-start.3
  537.8 5.4 copy-start.6
  541.1 87.9 %collective-permute-start.4 = (bf16[32,64,256]{2,1,0:T(8,128)(2,1)S(1)}, bf16[32,64,256]{2,1,0:T(8,128)(2,1)S(1)}, u32[]{:S(2)}, u32[]{:S(2)}) collective-permute-start(bf16[32,64,256]{2,1,0:T(8,128)(2,1)S(1)} %get-tuple-element.11), channel_id=1, source_target_pairs={{0,8},{4,12},{8,0},{12,4},{16,24},{20,28},{24,16},{28,20},{1,9},{5... | collective-permute-start | bytes 3145736 | tf_op jit(solution)/shard_map/ppermute | solution.py:13
  545.2 61.8 %collective-permute-start.5 = (f32[32]{0:T(128)S(1)}, f32[32]{0:T(128)S(1)}, u32[]{:S(2)}, u32[]{:S(2)}) collective-permute-start(f32[32]{0:T(128)S(1)} %get-tuple-element.10), channel_id=1, source_target_pairs={{0,8},{4,12},{8,0},{12,4},{16,24},{20,28},{24,16},{28,20},{1,9},{5... | collective-permute-start | bytes 392 | tf_op jit(solution)/shard_map/ppermute | solution.py:13
  607.6 20.9 %collective-permute-start.7 = (f32[32]{0:T(128)S(1)}, f32[32]{0:T(128)S(1)}, u32[]{:S(2)}, u32[]{:S(2)}) collective-permute-start(f32[32]{0:T(128)S(1)} %get-tuple-element.28), channel_id=1, source_target_pairs={{0,16},{4,20},{8,24},{12,28},{16,0},{20,4},{24,8},{28,12},{1,17},{... | collective-permute-start | bytes 392 | tf_op jit(solution)/shard_map/ppermute | solution.py:13
  629.4 18.4 %copy-start.5 = (f32[512,512]{1,0:T(8,128)S(1)}, f32[512,512]{1,0:T(8,128)}, u32[]{:S(2)}) copy-start(f32[512,512]{1,0:T(8,128)} %fusion.37) | copy-start | bytes 3145732
  629.5 18.4 %copy-start.7 = (f32[32,512]{1,0:T(8,128)S(1)}, f32[32,512]{1,0:T(8,128)}, u32[]{:S(2)}) copy-start(f32[32,512]{1,0:T(8,128)} %get-tuple-element.22) | copy-start | bytes 196612
  629.5 18.4 %collective-permute-start.6 = (bf16[8,64,256]{2,1,0:T(8,128)(2,1)S(1)}, bf16[8,64,256]{2,1,0:T(8,128)(2,1)}, u32[]{:S(2)}, u32[]{:S(2)}) collective-permute-start(bf16[8,64,256]{2,1,0:T(8,128)(2,1)S(1)} %select_convert_fusion.4), channel_id=1, source_target_pairs={{0,16},{4,20},{8,24},{12,28},{16,0},{20,4},{24,8},{28,12},{1,17},{... | collective-permute-start | bytes 786440 | tf_op jit(solution)/shard_map/ppermute | solution.py:13
  665.4 2.7 copy-start.14
  668.1 2.8 copy-start.13
  668.1 5.0 copy-start.11
  668.1 5.0 copy-start.12
  670.9 2.2 copy-start.4
  670.9 2.2 copy-start.8
  670.9 2.2 copy-start.9
  670.9 2.2 copy-start.10
  670.9 2.3 copy-start.16
  670.9 2.3 copy-start.17
  670.9 3.2 copy-start.3
  682.7 2.9 copy-start.1
Sparse Core Ops, SparseCore 0:
  88.4 87.7 all-gather.4
  177.8 148.0 all-gather.6
  327.4 193.4 all-gather.10
  648.0 17.0 all-gather.8
where the time goes:
time: 693 us; the launch traced here: 692 us
  waiting for transfers between devices  538 us (78%)
  matrix products  94.2 us (14%)
  local copies, waits for them, and re-layouts  22.1 us (3%)
  starting transfers between devices  15.9 us (2%)
  between operations  13.5 us (2%)
  other arithmetic  8.63 us (1%)
    all_gather x1, waiting for transfers between devices, on_device(): lax.all_gather(w_value, 'ctx', axis=0, tiled=True, axis_index_groups=groups)  150 us
    all_gather x1, waiting for transfers between devices, on_device(): rows = lax.all_gather(jnp.stack([kept, taken]), 'tp', axis=1, tiled=True)  86.4 us
    ppermute x2, waiting for transfers between devices, project(): back = lax.ppermute(other, 'ctx', across)  85.4 us
    ppermute x6, waiting for transfers between devices, swapped(): lax.ppermute(value, axis, [(i, i ^ 1 << distance) for i in range(lax.axis...  82.7 us
    all_gather x1, waiting for transfers between devices, on_device(): lax.all_gather(w_gate, 'ctx', axis=0, tiled=True, axis_index_groups=groups)  62.8 us
    ppermute x1, waiting for transfers between devices, on_device(): taken = lax.ppermute(given, 'ctx', across)  45.2 us
    dot_general x2, matrix products, project(): mine = jnp.dot(rows[0], weight, preferred_element_type=jnp.float32)  30.5 us
    dot_general x2, matrix products, project(): jnp.dot(rows[1], weight, preferred_element_type=jnp.float32)  29.2 us
  transfers between devices with their start and end apart: 14, of which 9 were waited for; matrix products, arithmetic and copies ran while one was open for 15% of the time, Pallas kernels for 0%

commit v1 on v0

--- a/solution.py
+++ b/solution.py
@@ -7,6 +7,24 @@
 STATE = 256
 HPG = 32
 LEVELS = 6
+
+
+def laid_out(blocks, dim):
+    lengths = list(blocks.shape[1:])
+    lengths[dim] *= blocks.shape[0]
+    return jnp.moveaxis(blocks, 0, dim).reshape(lengths)
+
+
+def grow_blocks(x, axis):
+    count = lax.axis_size(axis)
+    blocks = x[None]
+    for level in range(count.bit_length() - 1):
+        bit = 1 << level
+        other = lax.ppermute(blocks, axis, [(i, i ^ bit) for i in range(count)])
+        both = jnp.stack([blocks, other])
+        upper = lax.axis_index(axis) >> level & 1
+        blocks = jnp.where(upper == 0, both, both[::-1]).reshape(-1, *x.shape)
+    return blocks
 
 
 def swapped(value, axis, distance):
@@ -39,7 +57,8 @@
     kept = lax.dynamic_slice_in_dim(token_part, upper_half * depth, depth, 1)
     given = lax.dynamic_slice_in_dim(token_part, (1 - upper_half) * depth, depth, 1)
     taken = lax.ppermute(given, "ctx", across)
-    rows = lax.all_gather(jnp.stack([kept, taken]), "tp", axis=1, tiled=True)
+    x = jnp.stack([kept, taken])
+    rows = laid_out(grow_blocks(x, "tp"), 1)
     w_gate_half = lax.all_gather(w_gate, "ctx", axis=0, tiled=True, axis_index_groups=groups)
 
     def project(weight):

time: 693 us -> 579 us (0.84)
  waiting for transfers between devices: 538 us -> 377 us
  other arithmetic: 8.63 us -> 34.1 us
  local copies, waits for them, and re-layouts: 22.1 us -> 39.1 us
    all_gather x1, waiting for transfers between devices: 150 us -> 0.01 us  [on_device(): lax.all_gather(w_value, 'ctx', axis=0, tiled=True, axis_index_groups=groups)]
    ppermute x0 -> x2, waiting for transfers between devices: none -> 134 us  [grow_blocks(): other = lax.ppermute(blocks, axis, [(i, i ^ bit) for i in range(count)])]
    all_gather x1 -> x0, waiting for transfers between devices: 86.4 us -> none  [on_device(): rows = lax.all_gather(jnp.stack([kept, taken]), 'tp', axis=1, tiled=True)]
    all_gather x1, waiting for transfers between devices: 62.8 us -> 0.01 us  [on_device(): lax.all_gather(w_gate, 'ctx', axis=0, tiled=True, axis_index_groups=groups)]
    another operation x4 -> x7, other arithmetic: 3.42 us -> 17 us  [the longest x4 15.7 us: grow_blocks(): both = jnp.stack([blocks, other])]
    reshape x1 -> x2, local copies, waits for them, and re-layouts: 0.01 us -> 11.7 us  [the longest x1 11.7 us: grow_blocks(): blocks = jnp.where(upper == 0, both, both[::-1]).reshape(-1, *x.shape)]
    select_n x0 -> x1, other arithmetic: none -> 11.4 us  [grow_blocks(): blocks = jnp.where(upper == 0, both, both[::-1]).reshape(-1, *x.shape)]
    ppermute x6, waiting for transfers between devices: 82.7 us -> 90.4 us  [swapped(): lax.ppermute(value, axis, [(i, i ^ 1 << distance) for i in range(lax.axis...]
  transfers between devices with their start and end apart: 14 -> 15, of which waited for: 9 -> 8; matrix products, arithmetic and copies ran while one was open for 15% -> 25% of each run, Pallas kernels for 0% -> 0%
where the time goes in v1:
time: 579 us; the launch traced here: 574 us
  waiting for transfers between devices  377 us (65%)
  matrix products  90.8 us (16%)
  local copies, waits for them, and re-layouts  39.1 us (7%)
  other arithmetic  34.1 us (6%)
  starting transfers between devices  19.7 us (3%)
  between operations  13.4 us (2%)
    ppermute x2, waiting for transfers between devices, grow_blocks(): other = lax.ppermute(blocks, axis, [(i, i ^ bit) for i in range(count)])  134 us
    ppermute x6, waiting for transfers between devices, swapped(): lax.ppermute(value, axis, [(i, i ^ 1 << distance) for i in range(lax.axis...  90.4 us
    ppermute x2, waiting for transfers between devices, project(): back = lax.ppermute(other, 'ctx', across)  81.3 us
    ppermute x1, waiting for transfers between devices, on_device(): taken = lax.ppermute(given, 'ctx', across)  45.9 us
    dot_general x2, matrix products, project(): mine = jnp.dot(rows[0], weight, preferred_element_type=jnp.float32)  30.5 us
    dot_general x2, matrix products, project(): jnp.dot(rows[1], weight, preferred_element_type=jnp.float32)  29.5 us
    all_to_all x1, waiting for transfers between devices, on_device(): token_part = lax.all_to_all(hidden_rows, 'tp', 0, 1, tiled=True)  24.4 us
    another operation x4, other arithmetic, grow_blocks(): both = jnp.stack([blocks, other])  15.7 us
  transfers between devices with their start and end apart: 15, of which 8 were waited for; matrix products, arithmetic and copies ran while one was open for 25% of the time, Pallas kernels for 0%

profile of v1, /device:TPU:9, one launch (start us, length us, event | category | flops | bytes accessed | tf_op | source)
XLA Modules:
  0.0 574.3 jit_solution(6333102544470997937)
XLA Ops:
  8.0 3.6 all-to-all-start
  11.7 24.4 %all-to-all-done = bf16[4,128,2048]{2,1,0:T(8,128)(2,1)S(1)} async-done(((bf16[4,128,2048]{2,1,0:T(8,128)(2,1)}), bf16[4,128,2048]{2,1,0:T(8,128)(2,1)S(1)}, u32[]{:S(2)}, u32[]{:S(2)}) %all-to-all-start) | async-done | bytes 2097184 | tf_op jit(solution)/shard_map/all_to_all | solution.py:55
  37.4 3.1 copy.37
  40.7 2.3 collective-permute-start
  43.0 45.9 %collective-permute-done = bf16[128,4096]{0,1:T(8,128)(2,1)S(1)} collective-permute-done((bf16[128,4096]{0,1:T(8,128)(2,1)S(1)}, bf16[128,4096]{0,1:T(8,128)(2,1)S(1)}, u32[]{:S(2)}, u32[]{:S(2)}) %collective-permute-start) | collective-permute-done | bytes 1048608 | tf_op jit(solution)/shard_map/ppermute | solution.py:59
  91.1 45.0 %collective-permute-done.1 = bf16[1,2,128,4096]{2,3,1,0:T(8,128)(2,1)} collective-permute-done((bf16[1,2,128,4096]{2,3,1,0:T(8,128)(2,1)}, bf16[1,2,128,4096]{2,3,1,0:T(8,128)(2,1)}, u32[]{:S(2)}, u32[]{:S(2)}) %collective-permute-start.1) | collective-permute-done | bytes 2097184 | tf_op jit(solution)/shard_map/ppermute | solution.py:23
  138.0 4.4 fusion.9
  143.1 89.0 %collective-permute-done.2 = bf16[2,2,128,4096]{2,3,1,0:T(8,128)(2,1)} collective-permute-done((bf16[2,2,128,4096]{2,3,1,0:T(8,128)(2,1)}, bf16[2,2,128,4096]{2,3,1,0:T(8,128)(2,1)}, u32[]{:S(2)}, u32[]{:S(2)}) %collective-permute-start.2) | collective-permute-done | bytes 4194336 | tf_op jit(solution)/shard_map/ppermute | solution.py:23
  232.1 7.7 %pad_maximum_fusion = bf16[2,2,2,128,4096]{3,4,2,1,0:T(8,128)(2,1)} fusion(bf16[1,2,2,128,4096]{3,4,2,1,0:T(8,128)(2,1)} %bitcast.11, bf16[1,2,2,128,4096]{3,4,2,1,0:T(8,128)(2,1)} %get-tuple-element.13), kind=kLoop, calls=%fused_computation.6 | loop fusion | flops 4194304 | bytes 16777216 | tf_op jit(solution)/shard_map/stack | solution.py:24
  239.8 11.4 %reverse_select_fusion = bf16[2,2,2,128,4096]{3,4,2,1,0:T(8,128)(2,1)} fusion(bf16[2,2,2,128,4096]{3,4,2,1,0:T(8,128)(2,1)} %pad_maximum_fusion, pred[]{:T(512)S(6)} %eq.20), kind=kLoop, calls=%fused_computation.4 | loop fusion | flops 4194304 | bytes 16777216 | tf_op jit(solution)/shard_map/jit(_where)/select_n | solution.py:26
  251.2 11.7 %copy.38 = bf16[4,2,128,4096]{3,2,0,1:T(8,128)(2,1)} copy(bf16[4,2,128,4096]{2,3,1,0:T(8,128)(2,1)} %bitcast.91) | data formatting | bytes 16777216 | tf_op jit(solution)/shard_map/reshape | solution.py:26
  262.9 6.1 %fusion.47 = (bf16[1,4,128,4096]{3,2,1,0:T(8,128)(2,1)}, bf16[1,4,128,4096]{3,2,1,0:T(8,128)(2,1)}) fusion(bf16[2,4,128,4096]{3,2,1,0:T(8,128)(2,1)} %bitcast.92), kind=kLoop, calls=%fused_computation.94 | loop fusion | bytes 16777216 | tf_op jit(solution)/shard_map/slice | solution.py:65
  269.0 14.8 %convolution_convert_fusion.1 = bf16[512,2048]{1,0:T(8,128)(2,1)} fusion(bf16[512,4096]{1,0:T(8,128)(2,1)} %bitcast.99, bf16[4096,2048]{1,0:T(8,128)(2,1)} %all-gather.4.cloned.1.call-done), kind=kOutput, calls=%fused_computation.25 | convolution fusion | flops 8590983168 | bytes 23068672 | tf_op jit(solution)/shard_map/dot_general | solution.py:65
  285.9 3.6 collective-permute-start.5
  293.6 81.3 %collective-permute-done.3 = bf16[512,2048]{1,0:T(8,128)(2,1)} collective-permute-done((bf16[512,2048]{1,0:T(8,128)(2,1)}, bf16[512,2048]{1,0:T(8,128)(2,1)}, u32[]{:S(2)}, u32[]{:S(2)}) %collective-permute-start.3) | collective-permute-done | bytes 2097184 | tf_op jit(solution)/shard_map/ppermute | solution.py:66
  374.9 14.9 %add_convert_fusion.1 = bf16[512,2048]{1,0:T(8,128)(2,1)} fusion(bf16[512,2048]{1,0:T(8,128)(2,1)} %collective-permute-done.3, bf16[512,4096]{1,0:T(8,128)(2,1)} %bitcast.97, bf16[4096,2048]{1,0:T(8,128)(2,1)} %all-gather.4.cloned.1.call-done), kind=kOutput, calls=%fused_computation.18 | convolution fusion | flops 8593080320 | bytes 25165824 | tf_op jit(solution)/shard_map/dot_general | solution.py:67
  389.8 2.9 copy.39
  392.7 4.2 fusion.49
  396.9 3.0 collective-permute-start.4
  399.9 14.7 %convolution_convert_fusion = bf16[512,2048]{1,0:T(8,128)(2,1)} fusion(bf16[512,4096]{1,0:T(8,128)(2,1)} %bitcast.100, bf16[4096,2048]{1,0:T(8,128)(2,1)} %all-gather.8.cloned.1.call-done), kind=kOutput, calls=%fused_computation.24 | convolution fusion | flops 8590983168 | bytes 23068672 | tf_op jit(solution)/shard_map/dot_general | solution.py:65
  420.4 63.2 %collective-permute-done.7 = f32[32]{0:T(128)S(1)} collective-permute-done((f32[32]{0:T(128)S(1)}, f32[32]{0:T(128)S(1)}, u32[]{:S(2)}, u32[]{:S(2)}) %collective-permute-start.7) | collective-permute-done | bytes 160 | tf_op jit(solution)/shard_map/ppermute | solution.py:31
  486.0 19.1 %collective-permute-done.9 = f32[32]{0:T(128)S(1)} collective-permute-done((f32[32]{0:T(128)S(1)}, f32[32]{0:T(128)S(1)}, u32[]{:S(2)}, u32[]{:S(2)}) %collective-permute-start.9) | collective-permute-done | bytes 160 | tf_op jit(solution)/shard_map/ppermute | solution.py:31
  505.6 3.2 collective-permute-start.8
  508.8 2.7 fusion.18
  511.5 8.0 %collective-permute-done.8 = bf16[8,64,256]{2,1,0:T(8,128)(2,1)S(1)} collective-permute-done((bf16[8,64,256]{2,1,0:T(8,128)(2,1)S(1)}, bf16[8,64,256]{2,1,0:T(8,128)(2,1)S(1)}, u32[]{:S(2)}, u32[]{:S(2)}) %collective-permute-start.8) | collective-permute-done | bytes 262176 | tf_op jit(solution)/shard_map/ppermute | solution.py:31
  520.2 15.6 %fusion.13 = f32[512,2048]{1,0:T(8,128)} fusion(bf16[512,2048]{1,0:T(8,128)(2,1)} %collective-permute-done.10, bf16[512,4096]{1,0:T(8,128)(2,1)} %bitcast.98, bf16[4096,2048]{1,0:T(8,128)(2,1)} %all-gather.8.cloned.1.call-done), kind=kOutput, calls=%fused_computation.29 | convolution fusion | flops 8594128896 | bytes 27262976 | tf_op jit(solution)/shard_map/dot_general | solution.py:67
  535.8 5.4 copy.44
  541.2 2.7 fusion.19
  543.9 2.8 fusion.16
  546.8 2.1 fusion.17
  549.9 15.0 %multiply_reduce_fusion = (f32[512,32]{0,1:T(8,128)S(1)}, f32[512,32,64]{0,2,1:T(8,128)S(1)}) fusion(f32[512,32,64]{0,2,1:T(8,128)} %bitcast.96, bf16[512,32,64]{0,2,1:T(8,128)(2,1)S(1)} %bitcast.103, f32[32]{0:T(128)S(1)} %copy-done.17, f32[512,32]{0,1:T(8,128)S(1)} %copy-done.12, f32[512,32,64]{0,2,1:T(8,128)S(1)} %copy-done.3, ...), kind=kOutput, calls=%fused_computation.16 | convolution fusion | flops 1145028608 | bytes 29098112 | tf_op jit(solution)/shard_map/hts,shp->thp/dot_general | solution.py:85
  565.4 2.4 copy.45
  (86 shorter events, 24.8 us)
Async XLA Ops:
  6.5 277.2 %copy-start = (f32[512,32]{0,1:T(8,128)S(1)}, f32[512,32]{0,1:T(8,128)}, u32[]{:S(2)}) copy-start(f32[512,32]{0,1:T(8,128)} %param.13) | copy-start | bytes 196612
  6.5 262.4 %all-gather.4.cloned.1.call-start = ((), (), s32[]{:S(2)}) async-start(), calls=%async_computation.1 | async-start | bytes 20971520 | tf_op jit(solution)/shard_map/all_gather | solution.py:54
  7.3 392.7 %all-gather.8.cloned.1.call-start = ((), (), s32[]{:S(2)}) async-start(), calls=%async_computation.3 | async-start | bytes 20971520 | tf_op jit(solution)/shard_map/all_gather | solution.py:62
  8.0 28.1 %all-to-all-start = ((bf16[4,128,2048]{2,1,0:T(8,128)(2,1)}), bf16[4,128,2048]{2,1,0:T(8,128)(2,1)S(1)}, u32[]{:S(2)}, u32[]{:S(2)}) async-start(bf16[4,128,2048]{2,1,0:T(8,128)(2,1)} %bitcast.101), calls=%async_computation | async-start | bytes 4194304 | tf_op jit(solution)/shard_map/all_to_all | solution.py:55
  11.6 535.1 %all-gather.6.cloned.1.call-start = ((), (), s32[]{:S(2)}) async-start(), calls=%async_computation.2 | async-start | bytes 1310720 | tf_op jit(solution)/shard_map/all_gather | solution.py:111
  36.1 1.3 copy-start.2
  40.7 48.2 %collective-permute-start = (bf16[128,4096]{0,1:T(8,128)(2,1)S(1)}, bf16[128,4096]{0,1:T(8,128)(2,1)S(1)}, u32[]{:S(2)}, u32[]{:S(2)}) collective-permute-start(bf16[128,4096]{0,1:T(8,128)(2,1)S(1)} %get-tuple-element.20), channel_id=1, source_target_pairs={{0,16},{4,20},{8,24},{12,28},{16,0},{20,4},{24,8},{28,12},{1,17},{... | collective-permute-start | bytes 3145736 | tf_op jit(solution)/shard_map/ppermute | solution.py:59
  90.5 45.5 %collective-permute-start.1 = (bf16[1,2,128,4096]{2,3,1,0:T(8,128)(2,1)}, bf16[1,2,128,4096]{2,3,1,0:T(8,128)(2,1)}, u32[]{:S(2)}, u32[]{:S(2)}) collective-permute-start(bf16[1,2,128,4096]{2,3,1,0:T(8,128)(2,1)} %get-tuple-element.18), channel_id=1, source_target_pairs={{0,1},{1,0},{2,3},{3,2},{4,5},{5,4},{6,7},{7,6},{8,9},{9,8},{10,11... | collective-permute-start | bytes 6291464 | tf_op jit(solution)/shard_map/ppermute | solution.py:23
  142.4 89.6 %collective-permute-start.2 = (bf16[2,2,128,4096]{2,3,1,0:T(8,128)(2,1)}, bf16[2,2,128,4096]{2,3,1,0:T(8,128)(2,1)}, u32[]{:S(2)}, u32[]{:S(2)}) collective-permute-start(bf16[2,2,128,4096]{2,3,1,0:T(8,128)(2,1)} %get-tuple-element.14), channel_id=1, source_target_pairs={{0,2},{1,3},{2,0},{3,1},{4,6},{5,7},{6,4},{7,5},{8,10},{9,11},{10,... | collective-permute-start | bytes 12582920 | tf_op jit(solution)/shard_map/ppermute | solution.py:23
  269.0 20.6 %copy-start.5 = (bf16[512,2,4,256]{3,2,1,0:T(4,128)(2,1)S(1)}, bf16[512,2,4,256]{3,2,1,0:T(4,128)(2,1)}, u32[]{:S(2)}) copy-start(bf16[512,2,4,256]{3,2,1,0:T(4,128)(2,1)} %param.12) | copy-start | bytes 6291460
  283.8 91.2 %collective-permute-start.3 = (bf16[512,2048]{1,0:T(8,128)(2,1)}, bf16[512,2048]{1,0:T(8,128)(2,1)}, u32[]{:S(2)}, u32[]{:S(2)}) collective-permute-start(bf16[512,2048]{1,0:T(8,128)(2,1)} %convolution_convert_fusion.1), channel_id=1, source_target_pairs={{0,16},{4,20},{8,24},{12,28},{16,0},{20,4},{24,8},{28,12},{1,17},{... | collective-permute-start | bytes 6291464 | tf_op jit(solution)/shard_map/ppermute | solution.py:66
  285.1 5.7 copy-start.16
  285.9 128.7 %collective-permute-start.5 = (f32[32]{0:T(128)}, f32[32]{0:T(128)}, u32[]{:S(2)}, u32[]{:S(2)}) collective-permute-start(f32[32]{0:T(128)} %slice_reduce_fusion.1), channel_id=1, source_target_pairs={{0,4},{4,0},{8,12},{12,8},{16,20},{20,16},{24,28},{28,24},{1,5},{5... | collective-permute-start | bytes 392 | tf_op jit(solution)/shard_map/ppermute | solution.py:31
  389.8 2.9 copy-start.15
  392.7 4.3 copy-start.6
  396.9 18.4 %collective-permute-start.4 = (bf16[32,64,256]{2,1,0:T(8,128)(2,1)}, bf16[32,64,256]{2,1,0:T(8,128)(2,1)S(1)}, u32[]{:S(2)}, u32[]{:S(2)}) collective-permute-start(bf16[32,64,256]{2,1,0:T(8,128)(2,1)} %get-tuple-element.35), channel_id=1, source_target_pairs={{0,4},{4,0},{8,12},{12,8},{16,20},{20,16},{24,28},{28,24},{1,5},{5... | collective-permute-start | bytes 3145736 | tf_op jit(solution)/shard_map/ppermute | solution.py:31
  399.9 15.4 %copy-start.8 = (f32[32,64,256]{2,1,0:T(8,128)S(1)}, f32[32,64,256]{2,1,0:T(8,128)}, u32[]{:S(2)}) copy-start(f32[32,64,256]{2,1,0:T(8,128)} %get-tuple-element.36) | copy-start | bytes 6291460
  414.6 2.6 copy-start.10
  414.6 105.6 %collective-permute-start.10 = (bf16[512,2048]{1,0:T(8,128)(2,1)}, bf16[512,2048]{1,0:T(8,128)(2,1)}, u32[]{:S(2)}, u32[]{:S(2)}) collective-permute-start(bf16[512,2048]{1,0:T(8,128)(2,1)} %convolution_convert_fusion), channel_id=1, source_target_pairs={{0,16},{4,20},{8,24},{12,28},{16,0},{20,4},{24,8},{28,12},{1,17},{... | collective-permute-start | bytes 6291464 | tf_op jit(solution)/shard_map/ppermute | solution.py:66
  415.9 92.9 %copy-start.4 = (f32[32,64,256]{2,1,0:T(8,128)S(1)}, f32[32,64,256]{2,1,0:T(8,128)}, u32[]{:S(2)}) copy-start(f32[32,64,256]{2,1,0:T(8,128)} %param.15) | copy-start | bytes 6291460
  415.9 89.2 %collective-permute-start.6 = (bf16[32,64,256]{2,1,0:T(8,128)(2,1)S(1)}, bf16[32,64,256]{2,1,0:T(8,128)(2,1)S(1)}, u32[]{:S(2)}, u32[]{:S(2)}) collective-permute-start(bf16[32,64,256]{2,1,0:T(8,128)(2,1)S(1)} %get-tuple-element.9), channel_id=1, source_target_pairs={{0,8},{4,12},{8,0},{12,4},{16,24},{20,28},{24,16},{28,20},{1,9},{5... | collective-permute-start | bytes 3145736 | tf_op jit(solution)/shard_map/ppermute | solution.py:31
  419.3 64.3 %collective-permute-start.7 = (f32[32]{0:T(128)S(1)}, f32[32]{0:T(128)S(1)}, u32[]{:S(2)}, u32[]{:S(2)}) collective-permute-start(f32[32]{0:T(128)S(1)} %get-tuple-element.8), channel_id=1, source_target_pairs={{0,8},{4,12},{8,0},{12,4},{16,24},{20,28},{24,16},{28,20},{1,9},{5... | collective-permute-start | bytes 392 | tf_op jit(solution)/shard_map/ppermute | solution.py:31
  484.7 20.4 %collective-permute-start.9 = (f32[32]{0:T(128)S(1)}, f32[32]{0:T(128)S(1)}, u32[]{:S(2)}, u32[]{:S(2)}) collective-permute-start(f32[32]{0:T(128)S(1)} %get-tuple-element.32), channel_id=1, source_target_pairs={{0,16},{4,20},{8,24},{12,28},{16,0},{20,4},{24,8},{28,12},{1,17},{... | collective-permute-start | bytes 392 | tf_op jit(solution)/shard_map/ppermute | solution.py:31
  505.6 13.9 %collective-permute-start.8 = (bf16[8,64,256]{2,1,0:T(8,128)(2,1)S(1)}, bf16[8,64,256]{2,1,0:T(8,128)(2,1)S(1)}, u32[]{:S(2)}, u32[]{:S(2)}) collective-permute-start(bf16[8,64,256]{2,1,0:T(8,128)(2,1)S(1)} %select_convert_fusion.4), channel_id=1, source_target_pairs={{0,16},{4,20},{8,24},{12,28},{16,0},{20,4},{24,8},{28,12},{1,17},{... | collective-permute-start | bytes 786440 | tf_op jit(solution)/shard_map/ppermute | solution.py:31
  543.9 5.0 copy-start.9
  546.7 2.2 copy-start.7
  546.7 2.2 copy-start.12
  546.7 3.2 copy-start.3
  546.7 3.2 copy-start.13
  546.7 3.1 copy-start.14
  546.7 3.1 copy-start.17
  564.9 2.9 copy-start.1
  (1 other events, 0.7 us)
Sparse Core Ops, SparseCore 0:
  8.9 171.6 all-gather.3
  182.1 192.6 all-gather.7
  520.3 18.5 all-gather.5
